TPU v7x, 256 devices: a whole 4x4x8 slice. The times are simulated.
256 devices in a mesh: tm: 8 (over z_hi, y), aux: 32 (over z_lo, x, core).
Axes of the slice: x: 4, y: 4, z: 8 (z_hi: 2, z_lo: 4; z = z_hi * 4 + z_lo), core: 2. Of those that a mesh axis runs over, the one named last changes fastest.
Arguments:
- green: bfloat16 [16, 1024, 1024], P('tm'), may hold values from -4 to 4
- factors: bfloat16 [4096, 1024], P('aux'), may hold values from -0.1875 to 0.1875
- pattern: int32 [32, 8], P('aux'), may hold values 0 or 1
- coulomb: float32 [4096], P('aux'), may hold values from 0.5 to 2
Outputs:
- sigma: float32 [1024, 16, 1024], P('aux', 'tm')
All inputs are finite; a program needn't handle non-finite values. No bound on the sum of `pattern` on one device may be relied on, other than what follows from the above.
Results may differ from a plain program's by a relative error of at most 0.006.
Values may be sent and summed in bfloat16 or wider, within the bound.
No kernel may reach another device: no remote copies, remote signals or barrier semaphores. Data moves between devices by JAX's collectives and lax.ppermute only.
A program may use at most 64 MiB of HBM per device.

v0:
```python
import jax
import jax.numpy as jnp
from jax import lax
from jax.sharding import PartitionSpec as P

BLOCK = 128


def local(green, factors, pattern, coulomb):
    f32, bf16 = (jnp.float32, jnp.bfloat16)
    devices = lax.axis_size("aux")
    own = factors.shape[0]
    mask = jnp.repeat(jnp.repeat(pattern, BLOCK, axis=0), BLOCK, axis=1)
    masked = factors * mask.astype(factors.dtype)
    rows = lax.all_gather(masked, "aux", axis=0, tiled=True)
    left = jnp.einsum("qo,tok->tqk", masked, green, preferred_element_type=f32).astype(bf16)
    half = lax.axis_size("tm") // 2
    left = lax.ppermute(left, "tm", [(i, (i + half) % (2 * half)) for i in range(2 * half)])
    right = jnp.einsum("qo,tko->tqk", masked, green, preferred_element_type=f32).astype(bf16)
    weights = lax.all_gather(coulomb, "aux", axis=0, tiled=True)
    aux_green = jnp.einsum("tqo,po->tqp", right, rows, preferred_element_type=f32)
    mirror = jnp.einsum("tqo,po->tqp", left, rows, preferred_element_type=f32)
    kernel = aux_green * weights[None, None, :] * (aux_green * mirror) * coulomb[None, :, None]
    kernel = kernel.astype(bf16)
    part = jnp.einsum("tqp,pi->tqi", kernel, rows, preferred_element_type=f32).astype(bf16)
    times, orb = (green.shape[0], green.shape[1])
    part = part.reshape(times, own, devices, orb // devices).transpose(2, 0, 1, 3)
    part = lax.all_to_all(part, "aux", split_axis=0, concat_axis=0, tiled=True)
    rows = rows.reshape(devices, own, orb)
    return jnp.einsum("dtqi,dqj->itj", part, rows, preferred_element_type=f32)


def solution(mesh):
    in_specs = (P("tm", None, None), P("aux", None), P("aux", None), P("aux"))
    out_specs = P("aux", "tm", None)
    return jax.shard_map(local, mesh=mesh, in_specs=in_specs, out_specs=out_specs, check_vma=False)
```

profile of v0, /device:TPU:1, one launch (start us, length us, event | category | flops | bytes accessed | tf_op | source)
XLA Modules:
  0.0 154.6 jit_solution(5889969668802881452)
XLA Ops:
  6.5 0.0 copy-start.1
  6.5 0.0 all-gather.3.cloned.1.call-start
  6.5 0.7 convert_bitcast_fusion
  7.2 0.1 broadcast_bitcast_fusion
  7.3 1.7 %broadcast_multiply_fusion = bf16[128,1024]{1,0:T(8,128)(2,1)} fusion(bf16[128,1024]{1,0:T(8,128)(2,1)} %param.5, bf16[1024]{0:T(1024)(128)(2,1)S(1)} %broadcast_bitcast_fusion), kind=kLoop, calls=%fused_computation.20 | loop fusion | flops 131072 | bytes 526336 | tf_op jit(solution)/shard_map/mul | solution.py:14
  9.0 0.0 copy-start
  9.0 0.0 all-gather.3.cloned.1.call-update
  9.0 3.0 %fusion.28 = bf16[2,128,1024]{2,1,0:T(8,128)(2,1)S(1)} fusion(bf16[2,1024,1024]{2,1,0:T(8,128)(2,1)} %param.4, bf16[128,1024]{1,0:T(8,128)(2,1)} %broadcast_multiply_fusion), kind=kOutput, calls=%fused_computation.16 | convolution fusion | flops 537133056 | bytes 4980736 | tf_op jit(solution)/shard_map/qo,tok->tqk/dot_general | solution.py:16
  12.0 7.8 %collective-permute-start = (bf16[2,128,1024]{2,1,0:T(8,128)(2,1)S(1)}, bf16[2,128,1024]{2,1,0:T(8,128)(2,1)S(1)}, u32[]{:S(2)}, u32[]{:S(2)}) collective-permute-start(bf16[2,128,1024]{2,1,0:T(8,128)(2,1)S(1)} %fusion.28), channel_id=1, source_target_pairs={{0,128},{32,160},{64,192},{96,224},{128,0},{160,32},{192,64},{224,... | collective-permute-start | bytes 1572872 | tf_op jit(solution)/shard_map/ppermute | solution.py:18
  19.8 0.0 copy-done.1
  19.8 65.0 %all-gather = f32[32,1,128]{2,1,0:T(1,128)S(1)} all-gather(f32[1,1,128]{2,1,0:T(1,128)S(1)} %bitcast.62), channel_id=1, replica_groups=mesh['tm'=8,'aux'=32] {'aux'}, dimensions={0}, use_global_device_ids=true | all-gather | bytes 16896 | tf_op jit(solution)/shard_map/all_gather | solution.py:20
  84.8 12.6 %all-gather.3.cloned.1.call-done = bf16[4096,1024]{1,0:T(8,128)(2,1)} async-done(((bf16[128,1024]{1,0:T(8,128)(2,1)}), bf16[4096,1024]{1,0:T(8,128)(2,1)}) %all-gather.3.cloned.1.call-update) | async-done | bytes 8388624 | tf_op jit(solution)/shard_map/all_gather | solution.py:15
  97.4 0.0 copy-done
  97.4 10.4 %fusion.4 = f32[2,128,4096]{2,1,0:T(8,128)} fusion(bf16[4096,1024]{1,0:T(8,128)(2,1)} %all-gather.3.cloned.1.call-done, bf16[2,1024,1024]{2,1,0:T(8,128)(2,1)} %param.4, bf16[128,1024]{1,0:T(8,128)(2,1)S(1)} %copy-done), kind=kOutput, calls=%fused_computation.4 | convolution fusion | flops 2684616704 | bytes 17039360 | tf_op jit(solution)/shard_map/tqo,po->tqp/dot_general | solution.py:21
  107.8 0.0 collective-permute-done
  107.8 11.9 %fusion.22 = bf16[2,128,1024]{2,1,0:T(8,128)(2,1)S(1)} fusion(bf16[4096,1024]{1,0:T(8,128)(2,1)} %all-gather.3.cloned.1.call-done, f32[2,128,4096]{2,1,0:T(8,128)} %fusion.4, bf16[2,128,1024]{2,1,0:T(8,128)(2,1)S(1)} %collective-permute-done, f32[128]{0:T(128)S(1)} %copy-done.1, f32[4096]{0:T(1024)S(1)} %bitcast.61), kind=kOutput, calls=%fused_computation.12 | convolution fusion | flops 4300472320 | bytes 13648384 | tf_op jit(solution)/shard_map/tqp,pi->tqi/dot_general | solution.py:25
  119.6 0.3 copy.9
  119.9 0.1 copy.10
  120.0 21.9 %all_to_all.5 = bf16[32,2,128,32]{2,3,1,0:T(8,128)(2,1)S(1)} all-to-all(bf16[32,2,128,32]{2,3,1,0:T(8,128)(2,1)S(1)} %copy.10), channel_id=1, replica_groups=mesh['tm'=8,'aux'=32] {'aux'}, dimensions={0} | all-to-all | bytes 1048576 | tf_op jit(solution)/shard_map/all_to_all | solution.py:28
  141.9 5.0 %convolution_bitcast_fusion = f32[32,2,1024]{2,0,1:T(8,128)S(1)} fusion(bf16[32,128,1024,1]{2,1,3,0:T(8,128)(2,1)} %bitcast.63, bf16[32,2,128,32]{2,3,1,0:T(8,128)(2,1)S(1)} %all_to_all.5), kind=kOutput, calls=%fused_computation.17 | convolution fusion | flops 536870912 | bytes 9175040 | tf_op jit(solution)/shard_map/dtqi,dqj->itj/dot_general | solution.py:30
  146.9 0.9 copy.12
Async XLA Ops:
  6.5 13.3 %copy-start.1 = (f32[128]{0:T(128)S(1)}, f32[128]{0:T(128)}, u32[]{:S(2)}) copy-start(f32[128]{0:T(128)} %param.7) | copy-start | bytes 1540
  6.5 90.9 %all-gather.3.cloned.1.call-start = ((), (), s32[]{:S(2)}) async-start(), calls=%async_computation.1 | async-start | bytes 8650752 | tf_op jit(solution)/shard_map/all_gather | solution.py:15
  9.0 88.4 %copy-start = (bf16[128,1024]{1,0:T(8,128)(2,1)S(1)}, bf16[128,1024]{1,0:T(8,128)(2,1)}, u32[]{:S(2)}) copy-start(bf16[128,1024]{1,0:T(8,128)(2,1)} %broadcast_multiply_fusion) | copy-start | bytes 786436
  12.0 95.8 %collective-permute-start = (bf16[2,128,1024]{2,1,0:T(8,128)(2,1)S(1)}, bf16[2,128,1024]{2,1,0:T(8,128)(2,1)S(1)}, u32[]{:S(2)}, u32[]{:S(2)}) collective-permute-start(bf16[2,128,1024]{2,1,0:T(8,128)(2,1)S(1)} %fusion.28), channel_id=1, source_target_pairs={{0,128},{32,160},{64,192},{96,224},{128,0},{160,32},{192,64},{224,... | collective-permute-start | bytes 1572872 | tf_op jit(solution)/shard_map/ppermute | solution.py:18
Sparse Core Ops, SparseCore 0:
  9.2 88.1 all-gather.2
where the time goes:
time: 155 us
  blocking collectives  86.9 us (56%)
  matrix products  30.2 us (19%)
  between operations  13.4 us (9%)
  waiting for transfers between devices  12.6 us (8%)
  starting transfers between devices  7.83 us (5%)
  other arithmetic  2.34 us (2%)
    all_gather x1, blocking collectives, local(): weights = lax.all_gather(coulomb, 'aux', axis=0, tiled=True)  65 us
    all_to_all x1, blocking collectives, local(): part = lax.all_to_all(part, 'aux', split_axis=0, concat_axis=0, tiled=True)  21.9 us
    all_gather x1, waiting for transfers between devices, local(): rows = lax.all_gather(masked, 'aux', axis=0, tiled=True)  12.6 us
    dot_general x1, matrix products, local(): jnp.einsum('tqp,pi->tqi', kernel, rows, preferred_element_type=f32)  11.9 us
    dot_general x1, matrix products, local(): jnp.einsum('tqo,po->tqp', right, rows, preferred_element_type=f32)  10.4 us
    ppermute x1, starting transfers between devices, local(): lax.ppermute(left, 'tm', [(i, (i + half) % (2 * half)) for i in range(2 *...  7.83 us
    dot_general x1, matrix products, local(): return jnp.einsum('dtqi,dqj->itj', part, rows, preferred_element_type=f32)  4.96 us
  transfers between devices with their start and end apart: 2, of which 1 were waited for; matrix products, arithmetic and copies ran while one was open for 9% of the time, Pallas kernels for 0%

commit v1 on v0

--- a/solution.py
+++ b/solution.py
@@ -12,7 +12,9 @@
     own = factors.shape[0]
     mask = jnp.repeat(jnp.repeat(pattern, BLOCK, axis=0), BLOCK, axis=1)
     masked = factors * mask.astype(factors.dtype)
-    rows = lax.all_gather(masked, "aux", axis=0, tiled=True)
+    rows = jnp.concatenate(
+        lax.all_to_all(jnp.stack([masked] * lax.axis_size("aux")), "aux", 0, 0), axis=0
+    )
     left = jnp.einsum("qo,tok->tqk", masked, green, preferred_element_type=f32).astype(bf16)
     half = lax.axis_size("tm") // 2
     left = lax.ppermute(left, "tm", [(i, (i + half) % (2 * half)) for i in range(2 * half)])

time: 155 us -> 299 us (1.93)
  blocking collectives: 86.9 us -> 239 us
  between operations: 13.4 us -> 0.06 us
  starting transfers between devices: 7.83 us -> 14.4 us
  waiting for transfers between devices: 12.6 us -> 8.29 us
  local copies, waits for them, and re-layouts: 1.32 us -> 5.61 us
    all_gather x1, blocking collectives: 65 us -> 192 us  [local(): weights = lax.all_gather(coulomb, 'aux', axis=0, tiled=True)]
    all_to_all x1, blocking collectives: 21.9 us -> 46.4 us  [local(): part = lax.all_to_all(part, 'aux', split_axis=0, concat_axis=0, tiled=True)]
    all_gather x1 -> x0, waiting for transfers between devices: 12.6 us -> none  [local(): rows = lax.all_gather(masked, 'aux', axis=0, tiled=True)]
    all_to_all x0 -> x1, starting transfers between devices: none -> 10.1 us  [local(): lax.all_to_all(jnp.stack([masked] * lax.axis_size('aux')), 'aux', 0, 0)]
    all_to_all x0 -> x1, waiting for transfers between devices: none -> 8.29 us  [local(): lax.all_to_all(jnp.stack([masked] * lax.axis_size('aux')), 'aux', 0, 0)]
    another operation x0 -> x1, local copies, waits for them, and re-layouts: none -> 4.3 us  [local(): jnp.stack([masked] * lax.axis_size('aux'))]
    ppermute x1, starting transfers between devices: 7.83 us -> 4.3 us  [local(): lax.ppermute(left, 'tm', [(i, (i + half) % (2 * half)) for i in range(2 *...]
  transfers between devices with their start and end apart: 2 -> 2, of which waited for: 1 -> 1; matrix products, arithmetic and copies ran while one was open for 9% -> 4% of each run, Pallas kernels for 0% -> 0%
where the time goes in v1:
time: 299 us
  blocking collectives  239 us (80%)
  matrix products  30.1 us (10%)
  starting transfers between devices  14.4 us (5%)
  waiting for transfers between devices  8.29 us (3%)
  local copies, waits for them, and re-layouts  5.61 us (2%)
    all_gather x1, blocking collectives, local(): weights = lax.all_gather(coulomb, 'aux', axis=0, tiled=True)  192 us
    all_to_all x1, blocking collectives, local(): part = lax.all_to_all(part, 'aux', split_axis=0, concat_axis=0, tiled=True)  46.4 us
    dot_general x1, matrix products, local(): jnp.einsum('tqp,pi->tqi', kernel, rows, preferred_element_type=f32)  11.9 us
    dot_general x1, matrix products, local(): jnp.einsum('tqo,po->tqp', right, rows, preferred_element_type=f32)  10.4 us
    all_to_all x1, starting transfers between devices, local(): lax.all_to_all(jnp.stack([masked] * lax.axis_size('aux')), 'aux', 0, 0)  10.1 us
    all_to_all x1, waiting for transfers between devices, local(): lax.all_to_all(jnp.stack([masked] * lax.axis_size('aux')), 'aux', 0, 0)  8.29 us
  transfers between devices with their start and end apart: 2, of which 1 were waited for; matrix products, arithmetic and copies ran while one was open for 4% of the time, Pallas kernels for 0%

profile of v1, /device:TPU:1, one launch (start us, length us, event | category | flops | bytes accessed | tf_op | source)
XLA Modules:
  0.0 298.7 jit_solution(8266163382021103572)
XLA Ops:
  0.0 0.7 convert_bitcast_fusion
  0.7 0.1 broadcast_bitcast_fusion
  0.7 1.0 broadcast_multiply_fusion
  1.7 4.3 %stack.2 = bf16[32,128,1024]{2,1,0:T(8,128)(2,1)} broadcast(bf16[128,1024]{1,0:T(8,128)(2,1)S(1)} %broadcast_multiply_fusion), dimensions={1,2} | broadcast | bytes 8650752 | tf_op jit(solution)/shard_map/stack | solution.py:16
  6.0 10.1 %all-to-all-start = ((bf16[32,128,1024]{2,1,0:T(8,128)(2,1)}), bf16[32,128,1024]{2,1,0:T(8,128)(2,1)}, u32[]{:S(2)}, u32[]{:S(2)}) async-start(bf16[32,128,1024]{2,1,0:T(8,128)(2,1)} %stack.2), calls=%async_computation | async-start | bytes 16777216 | tf_op jit(solution)/shard_map/all_to_all | solution.py:16
  16.1 0.0 copy-start
  16.1 2.9 fusion.6
  19.0 4.3 %collective-permute-start = (bf16[2,128,1024]{2,1,0:T(8,128)(2,1)S(1)}, bf16[2,128,1024]{2,1,0:T(8,128)(2,1)S(1)}, u32[]{:S(2)}, u32[]{:S(2)}) collective-permute-start(bf16[2,128,1024]{2,1,0:T(8,128)(2,1)S(1)} %fusion.6), channel_id=1, source_target_pairs={{0,128},{32,160},{64,192},{96,224},{128,0},{160,32},{192,64},{224,... | collective-permute-start | bytes 1572872 | tf_op jit(solution)/shard_map/ppermute | solution.py:20
  23.3 0.0 copy-done
  23.3 192.2 %all-gather = f32[32,1,128]{2,1,0:T(1,128)S(1)} all-gather(f32[1,1,128]{2,1,0:T(1,128)S(1)} %bitcast.48), channel_id=1, replica_groups=mesh['tm'=8,'aux'=32] {'aux'}, dimensions={0}, use_global_device_ids=true | all-gather | bytes 16896 | tf_op jit(solution)/shard_map/all_gather | solution.py:22
  215.5 8.3 %all-to-all-done = bf16[32,128,1024]{2,1,0:T(8,128)(2,1)} async-done(((bf16[32,128,1024]{2,1,0:T(8,128)(2,1)}), bf16[32,128,1024]{2,1,0:T(8,128)(2,1)}, u32[]{:S(2)}, u32[]{:S(2)}) %all-to-all-start) | async-done | bytes 8388640 | tf_op jit(solution)/shard_map/all_to_all | solution.py:16
  223.8 10.4 %fusion.10 = f32[2,128,4096]{2,1,0:T(8,128)} fusion(bf16[4096,1024,1]{1,0,2:T(8,128)(2,1)} %bitcast.5, bf16[2,1024,1024]{2,1,0:T(8,128)(2,1)} %param.4, bf16[128,1024]{1,0:T(8,128)(2,1)S(1)} %broadcast_multiply_fusion), kind=kOutput, calls=%fused_computation.12 | convolution fusion | flops 2684616704 | bytes 17039360 | tf_op jit(solution)/shard_map/tqo,po->tqp/dot_general | solution.py:23
  234.2 0.0 collective-permute-done
  234.2 11.9 %convolution_convert_fusion = bf16[2,128,1024]{2,1,0:T(8,128)(2,1)S(1)} fusion(bf16[4096,1024,1]{1,0,2:T(8,128)(2,1)} %bitcast.5, f32[2,128,4096]{2,1,0:T(8,128)} %fusion.10, bf16[2,128,1024]{2,1,0:T(8,128)(2,1)S(1)} %collective-permute-done, f32[128]{0:T(128)S(1)} %copy-done, f32[4096]{0:T(1024)S(1)} %bitcast.47), kind=kOutput, calls=%fused_computation.6 | convolution fusion | flops 4300472320 | bytes 13648384 | tf_op jit(solution)/shard_map/tqp,pi->tqi/dot_general | solution.py:27
  246.1 0.3 copy.9
  246.4 0.1 copy.10
  246.4 46.4 %all_to_all.10 = bf16[32,2,128,32]{2,3,1,0:T(8,128)(2,1)S(1)} all-to-all(bf16[32,2,128,32]{2,3,1,0:T(8,128)(2,1)S(1)} %copy.10), channel_id=1, replica_groups=mesh['tm'=8,'aux'=32] {'aux'}, dimensions={0} | all-to-all | bytes 1048576 | tf_op jit(solution)/shard_map/all_to_all | solution.py:30
  292.8 5.0 %fusion.7 = f32[32,2,1024]{2,0,1:T(8,128)S(1)} fusion(bf16[32,2,128,32]{2,3,1,0:T(8,128)(2,1)S(1)} %all_to_all.10, bf16[32,128,1024]{2,1,0:T(8,128)(2,1)} %all-to-all-done), kind=kOutput, calls=%fused_computation.11 | convolution fusion | flops 536870912 | bytes 9175040 | tf_op jit(solution)/shard_map/dtqi,dqj->itj/dot_general | solution.py:32
  297.8 0.9 copy.12
Async XLA Ops:
  6.0 217.8 %all-to-all-start = ((bf16[32,128,1024]{2,1,0:T(8,128)(2,1)}), bf16[32,128,1024]{2,1,0:T(8,128)(2,1)}, u32[]{:S(2)}, u32[]{:S(2)}) async-start(bf16[32,128,1024]{2,1,0:T(8,128)(2,1)} %stack.2), calls=%async_computation | async-start | bytes 16777216 | tf_op jit(solution)/shard_map/all_to_all | solution.py:16
  16.1 7.2 %copy-start = (f32[128]{0:T(128)S(1)}, f32[128]{0:T(128)}, u32[]{:S(2)}) copy-start(f32[128]{0:T(128)} %param.7) | copy-start | bytes 1540
  19.0 215.2 %collective-permute-start = (bf16[2,128,1024]{2,1,0:T(8,128)(2,1)S(1)}, bf16[2,128,1024]{2,1,0:T(8,128)(2,1)S(1)}, u32[]{:S(2)}, u32[]{:S(2)}) collective-permute-start(bf16[2,128,1024]{2,1,0:T(8,128)(2,1)S(1)} %fusion.6), channel_id=1, source_target_pairs={{0,128},{32,160},{64,192},{96,224},{128,0},{160,32},{192,64},{224,... | collective-permute-start | bytes 1572872 | tf_op jit(solution)/shard_map/ppermute | solution.py:20
